TPU v7x, 32 devices: a whole 2x2x4 slice. The times are simulated.
32 devices in a mesh: space: 16 (over z, x, core), mem: 2 (over y).
Axes of the slice: x: 2, y: 2, z: 4, core: 2. Of those that a mesh axis runs over, the one named last changes fastest.
Arguments:
- ensemble: bfloat16 [8, 32, 512, 1536], P('mem', None, 'space'), may hold values from -12 to 12
- vector: bfloat16 [32, 512, 1536], P(None, 'space'), may hold values from -6 to 6
- modes: float32 [16, 32], replicated, may hold values from -1 to 1
- legendre: bfloat16 [512, 512, 256], P('space'), may hold values from -0.25 to 0.25
- spectrum: float32 [512, 256], P('space'), may hold values from 0.1 to 1
- truncation: int32 [1], replicated, may hold values from 543 to 702
Outputs:
- covariance_apply: bfloat16 [32, 512, 1536], P(None, 'space')
All inputs are finite; a program needn't handle non-finite values.
Results may differ from a plain program's by a relative error of at most 0.014.
Values may be sent and summed in bfloat16 or wider, within the bound.
A program may use at most 128 MiB of HBM per device.

v0:
```python
import math
import jax
import jax.numpy as jnp
from jax import lax
from jax.sharding import PartitionSpec as P

NMODE = 16
NLON = 1536
M = 512
NDEG = 256


def fourier_table(length, wave_count):
    points = jnp.arange(length, dtype=jnp.int32)
    orders = jnp.arange(wave_count, dtype=jnp.int32)
    phases = points[:, None] * orders[None, :] % length
    angles = phases.astype(jnp.float32) * (2.0 * math.pi / length)
    amplitude = math.sqrt(2.0 / length)
    stacked = jnp.stack([jnp.cos(angles), -jnp.sin(angles)], axis=-1) * amplitude
    return stacked.reshape(length, 2 * wave_count).astype(jnp.bfloat16)


def on_device(ensemble, vector, modes, legendre, spectrum, truncation):
    members = ensemble.shape[0]
    lat_rows = ensemble.shape[2]
    own_waves = legendre.shape[0]
    sources = lax.axis_size("space")
    total_members = members * lax.axis_size("mem")
    highest = lax.Precision.HIGHEST
    fourier = fourier_table(NLON, M)
    product = ensemble.astype(jnp.float32) * vector.astype(jnp.float32)[None]
    projected = jnp.einsum("jl,klac->kjac", modes, product, precision=highest).astype(jnp.bfloat16)
    fields = members * NMODE
    columns = fields * lat_rows
    zonal_parts = lax.dot_general(
        fourier,
        projected.reshape(columns, NLON),
        (((0,), (1,)), ((), ())),
        preferred_element_type=jnp.float32,
    )
    zonal_parts = zonal_parts.astype(jnp.bfloat16).reshape(1, 2 * M, columns)
    first_wave = lax.axis_index("space") * own_waves
    wavenumber = (
        first_wave
        + jnp.arange(own_waves, dtype=jnp.int32)[:, None]
        + jnp.arange(NDEG, dtype=jnp.int32)[None, :]
    )
    factor = jnp.where(wavenumber <= truncation[0], spectrum, jnp.zeros_like(spectrum))
    arrived = lax.all_to_all(zonal_parts, "space", split_axis=1, concat_axis=0, tiled=True)
    arrived = arrived.reshape(sources, own_waves, 2, fields, lat_rows)
    legendre_view = legendre.reshape(own_waves, sources, lat_rows, NDEG)
    harmonic = jnp.einsum(
        "smrfa,msan->mrfn", arrived, legendre_view, preferred_element_type=jnp.float32
    )
    weighted = (harmonic * factor[:, None, None, :]).astype(jnp.bfloat16)
    synthesis = jnp.einsum(
        "mrfn,msan->smrfa", weighted, legendre_view, preferred_element_type=jnp.float32
    )
    synthesis = synthesis.astype(jnp.bfloat16).reshape(sources, 2 * own_waves, columns)
    returned = lax.all_to_all(synthesis, "space", split_axis=0, concat_axis=1, tiled=True)
    spread = lax.dot_general(
        returned.reshape(2 * M, columns),
        fourier,
        (((0,), (1,)), ((), ())),
        preferred_element_type=jnp.float32,
    )
    spread = spread.reshape(members, NMODE, lat_rows, NLON)
    lifted = jnp.einsum("jl,kjac->klac", modes, spread, precision=highest)
    partial_value = jnp.sum(ensemble.astype(jnp.float32) * lifted, axis=0)
    summed = lax.psum(partial_value.astype(jnp.bfloat16), "mem").astype(jnp.float32)
    return (summed / (total_members - 1)).astype(jnp.bfloat16)


def solution(mesh):
    placed = (
        P("mem", None, "space", None),
        P(None, "space", None),
        P(),
        P("space", None, None),
        P("space", None),
        P(),
    )
    return jax.shard_map(
        on_device, mesh=mesh, in_specs=placed, out_specs=P(None, "space", None), check_vma=False
    )
```

profile of v0, /device:TPU:0, one launch (start us, length us, event | category | flops | bytes accessed | tf_op | source)
XLA Modules:
  0.0 595.8 jit_solution(11271373535638854482)
XLA Ops:
  6.5 12.9 %sine_negate_fusion = (f32[1536,512,1]{1,0,2:T(8,128)S(1)}, f32[1536,512,1]{1,0,2:T(8,128)S(1)}) fusion(), kind=kLoop, calls=%fused_computation.23 | loop fusion | flops 7864320 | bytes 6291456 | tf_op jit(solution)/shard_map/neg | solution.py:19
  21.3 19.5 %convert_bitcast_fusion.1 = bf16[4,16,32,1536]{3,1,2,0:T(8,128)(2,1)S(1)} fusion(f32[32,32,1536]{2,0,1:T(8,128)S(1)} %copy.28, bf16[4,32,32,1536]{3,2,1,0:T(8,128)(2,1)S(1)} %copy-done.1, f32[16,32]{1,0:T(8,128)S(1)} %copy-done), kind=kOutput, calls=%fused_computation.13 | convolution fusion | flops 1223688192 | bytes 25167872 | tf_op jit(solution)/shard_map/jl,klac->kjac/dot_general | solution.py:32
  40.8 6.1 %copy.29 = bf16[4,16,32,1536]{3,2,1,0:T(8,128)(2,1)} copy(bf16[4,16,32,1536]{3,1,2,0:T(8,128)(2,1)S(1)} %convert_bitcast_fusion.1) | data formatting | bytes 12582912 | tf_op jit(solution)/shard_map/convert_element_type | solution.py:32
  49.5 7.4 %copy.27 = bf16[1536,512,2]{0,2,1:T(2,128)(2,1)S(1)} copy(bf16[1536,512,2]{1,0,2:T(8,128)(2,1)} %fusion.7) | data formatting | bytes 6291456 | tf_op jit(solution)/shard_map/convert_element_type | solution.py:20
  59.6 10.0 %convert_bitcast_fusion.2 = bf16[1,1024,2048]{2,1,0:T(8,128)(2,1)S(1)} fusion(bf16[1536,1024]{0,1:T(8,128)(2,1)} %convert_element_type.69, bf16[2048,1536]{1,0:T(8,128)(2,1)} %bitcast.60), kind=kOutput, calls=%fused_computation.19 | convolution fusion | flops 6444548096 | bytes 13631488 | tf_op jit(solution)/shard_map/dot_general | solution.py:35
  69.6 24.6 %copy.67 = bf16[1,1024,2048]{2,0,1:T(2,128)(2,1)} copy(bf16[1,1024,2048]{2,1,0:T(8,128)(2,1)S(1)} %convert_bitcast_fusion.2) | data formatting | bytes 8388608 | tf_op jit(solution)/shard_map/reshape | solution.py:41
  94.8 27.4 %reduce.2 = bf16[1024,2048]{1,0:T(8,128)(2,1)} reduce(bf16[1024,1,2048]{2,1,0:T(2,128)(2,1)} %bitcast.56, bf16[]{:T(256)} %broadcast.88), dimensions={1}, to_apply=%bitcast.54.reduce_sub_computation | reduce | bytes 8388610
  122.1 11.4 %reshape.117 = bf16[16,2,65536]{2,1,0:T(2,128)(2,1)} reshape(bf16[1024,2048]{1,0:T(8,128)(2,1)} %reduce.2) | data formatting | bytes 8388608
  133.5 7.6 %all-to-all-start = ((bf16[16,2,65536]{2,1,0:T(2,128)(2,1)}), bf16[16,2,65536]{2,1,0:T(2,128)(2,1)}, u32[]{:S(2)}, u32[]{:S(2)}) async-start(bf16[16,2,65536]{2,1,0:T(2,128)(2,1)} %reshape.117), calls=%async_computation | async-start | bytes 8388608 | tf_op jit(solution)/shard_map/all_to_all | solution.py:49
  141.9 76.7 %all-to-all-done = bf16[16,2,65536]{2,1,0:T(2,128)(2,1)} async-done(((bf16[16,2,65536]{2,1,0:T(2,128)(2,1)}), bf16[16,2,65536]{2,1,0:T(2,128)(2,1)}, u32[]{:S(2)}, u32[]{:S(2)}) %all-to-all-start) | async-done | bytes 4194336 | tf_op jit(solution)/shard_map/all_to_all | solution.py:49
  218.6 12.7 %reshape.118 = bf16[1024,1,2048]{2,1,0:T(2,128)(2,1)} reshape(bf16[16,2,65536]{2,1,0:T(2,128)(2,1)} %all-to-all-done) | data formatting | bytes 8388608
  231.3 27.3 %bitcast_reduce_fusion = bf16[1024,2048]{1,0:T(8,128)(2,1)} fusion(bf16[1024,1,2048]{2,1,0:T(2,128)(2,1)} %reshape.118), kind=kLoop, calls=%fused_computation.36 | loop fusion | bytes 8388608 | tf_op jit(solution)/shard_map/all_to_all | solution.py:49
  258.6 19.5 %reshape.106 = bf16[16,32,2,64,32]{4,3,2,1,0:T(8,128)(2,1)} reshape(bf16[1024,2048]{1,0:T(8,128)(2,1)} %bitcast_reduce_fusion) | data formatting | bytes 8388608 | tf_op jit(solution)/shard_map/reshape | solution.py:50
  278.1 10.1 %fusion.2 = f32[32,2,64,256,1]{3,2,0,1,4:T(8,128)S(1)} fusion(bf16[16,32,2,64,32]{4,3,2,1,0:T(8,128)(2,1)} %reshape.106, bf16[32,16,32,256,1]{3,2,1,0,4:T(8,128)(2,1)} %bitcast.58), kind=kOutput, calls=%fused_computation.4 | convolution fusion | flops 1073741824 | bytes 16777216 | tf_op jit(solution)/shard_map/smrfa,msan->mrfn/dot_general | solution.py:52
  288.2 10.0 %convert_bitcast_fusion = bf16[16,32,2,64,32]{3,4,0,2,1:T(8,128)(2,1)} fusion(bf16[32,16,32,256,1]{3,2,1,4,0:T(8,128)(2,1)} %bitcast.59, f32[32,2,64,256,1]{3,2,0,1,4:T(8,128)S(1)} %fusion.2, f32[32,256]{1,0:T(8,128)S(1)} %fusion.21), kind=kOutput, calls=%fused_computation.9 | convolution fusion | flops 1077936128 | bytes 16809984 | tf_op jit(solution)/shard_map/mrfn,msan->smrfa/dot_general | solution.py:56
  298.3 15.9 %copy.33 = bf16[16,32,2,64,32]{4,3,2,1,0:T(8,128)(2,1)} copy(bf16[16,32,2,64,32]{3,4,0,2,1:T(8,128)(2,1)} %convert_bitcast_fusion) | data formatting | bytes 8388608 | tf_op jit(solution)/shard_map/convert_element_type | solution.py:59
  314.2 22.6 %reshape.108 = bf16[16,64,2048]{2,1,0:T(8,128)(2,1)} reshape(bf16[16,32,2,64,32]{4,3,2,1,0:T(8,128)(2,1)} %copy.33) | data formatting | bytes 8388608 | tf_op jit(solution)/shard_map/reshape | solution.py:59
  336.7 112.0 %all_to_all.8 = bf16[16,64,2048]{2,1,0:T(8,128)(2,1)} all-to-all(bf16[16,64,2048]{2,1,0:T(8,128)(2,1)} %reshape.108), channel_id=1, replica_groups=mesh['space'=16,'mem'=2] {'space'}, dimensions={0} | all-to-all | bytes 8388608 | tf_op jit(solution)/shard_map/all_to_all | solution.py:60
  448.8 6.6 %copy.34 = bf16[1024,2048]{0,1:T(8,128)(2,1)} copy(bf16[1024,2048]{1,0:T(8,128)(2,1)} %bitcast.57) | data formatting | bytes 8388608 | tf_op jit(solution)/shard_map/reshape | solution.py:62
  455.3 9.5 %fusion.9 = f32[4,16,32,1536]{3,1,2,0:T(8,128)S(1)} fusion(bf16[4,16,32,1024]{3,2,1,0:T(8,128)(2,1)} %bitcast.61, bf16[1536,1024]{0,1:T(8,128)(2,1)S(1)} %copy-done.2), kind=kOutput, calls=%fused_computation.17 | convolution fusion | flops 6442450944 | bytes 19922944 | tf_op jit(solution)/shard_map/dot_general | solution.py:61
  464.8 31.1 %fusion.1 = bf16[32,32,1536]{2,0,1:T(8,128)(2,1)} fusion(f32[4,16,32,1536]{3,1,2,0:T(8,128)S(1)} %fusion.9, bf16[4,32,32,1536]{3,2,1,0:T(8,128)(2,1)} %param.6, f32[16,32]{1,0:T(8,128)S(1)} %copy-done), kind=kOutput, calls=%fused_computation.3 | convolution fusion | flops 1225261056 | bytes 28313600 | tf_op jit(solution)/shard_map/jl,kjac->klac/dot_general | solution.py:68
  496.0 86.7 %all-reduce.2.cloned.1.call-done = bf16[32,32,1536]{2,0,1:T(8,128)(2,1)} async-done(((bf16[32,32,1536]{2,0,1:T(8,128)(2,1)}), bf16[32,32,1536]{2,0,1:T(8,128)(2,1)}) %all-reduce.2.cloned.1.call-update) | async-done | bytes 3145744 | tf_op jit(solution)/shard_map/psum | solution.py:70
  582.6 2.7 multiply_convert_fusion
  585.3 3.4 copy.37
  (18 shorter events, 7.7 us)
Async XLA Ops:
  6.5 14.8 %copy-start = (f32[16,32]{1,0:T(8,128)S(1)}, f32[16,32]{1,0:T(8,128)}, u32[]{:S(2)}) copy-start(f32[16,32]{1,0:T(8,128)} %param.8) | copy-start | bytes 6148
  6.5 12.9 %copy-start.3 = (bf16[32,32,1536]{2,1,0:T(8,128)(2,1)S(1)}, bf16[32,32,1536]{2,1,0:T(8,128)(2,1)}, u32[]{:S(2)}) copy-start(bf16[32,32,1536]{2,1,0:T(8,128)(2,1)} %param.7) | copy-start | bytes 9437188
  6.5 14.8 %copy-start.1 = (bf16[4,32,32,1536]{3,2,1,0:T(8,128)(2,1)S(1)}, bf16[4,32,32,1536]{3,2,1,0:T(8,128)(2,1)}, u32[]{:S(2)}) copy-start(bf16[4,32,32,1536]{3,2,1,0:T(8,128)(2,1)} %param.6) | copy-start | bytes 37748740
  133.5 8.3 %copy-start.4 = (f32[32,256]{1,0:T(8,128)S(1)}, f32[32,256]{1,0:T(8,128)}, u32[]{:S(2)}) copy-start(f32[32,256]{1,0:T(8,128)} %param.10) | copy-start | bytes 98308
  133.5 85.1 %all-to-all-start = ((bf16[16,2,65536]{2,1,0:T(2,128)(2,1)}), bf16[16,2,65536]{2,1,0:T(2,128)(2,1)}, u32[]{:S(2)}, u32[]{:S(2)}) async-start(bf16[16,2,65536]{2,1,0:T(2,128)(2,1)} %reshape.117), calls=%async_computation | async-start | bytes 8388608 | tf_op jit(solution)/shard_map/all_to_all | solution.py:49
  141.1 441.5 %all-reduce.2.cloned.1.call-start = ((), (), s32[]{:S(2)}) async-start(), calls=%async_computation.2 | async-start | bytes 6291456 | tf_op jit(solution)/shard_map/psum | solution.py:70
  448.8 6.6 %copy-start.2 = (bf16[1536,1024]{0,1:T(8,128)(2,1)S(1)}, bf16[1536,1024]{0,1:T(8,128)(2,1)}, u32[]{:S(2)}) copy-start(bf16[1536,1024]{0,1:T(8,128)(2,1)} %convert_element_type.69) | copy-start | bytes 9437188
Sparse Core Ops, SparseCore 0:
  496.1 86.5 all-reduce.1
where the time goes:
time: 607 us; the launch traced here: 596 us
  local copies, waits for them, and re-layouts  163 us (27%)
  waiting for transfers between devices  163 us (27%)
  blocking collectives  112 us (18%)
  matrix products  90.2 us (15%)
  other arithmetic  45.6 us (8%)
  between operations  14.4 us (2%)
  starting transfers between devices  7.61 us (1%)
    all_to_all x1, blocking collectives, on_device(): lax.all_to_all(synthesis, 'space', split_axis=0, concat_axis=1, tiled=True)  112 us
    psum x1, waiting for transfers between devices, on_device(): lax.psum(partial_value.astype(jnp.bfloat16), 'mem').astype(jnp.float32)  86.7 us
    all_to_all x1, waiting for transfers between devices, on_device(): lax.all_to_all(zonal_parts, 'space', split_axis=1, concat_axis=0, tiled=T...  76.7 us
    dot_general x1, matrix products, on_device(): lifted = jnp.einsum('jl,kjac->klac', modes, spread, precision=highest)  31.1 us
    unnamed x1, other arithmetic  27.4 us
    all_to_all x1, local copies, waits for them, and re-layouts, on_device(): lax.all_to_all(zonal_parts, 'space', split_axis=1, concat_axis=0, tiled=T...  27.3 us
    reshape x1, local copies, waits for them, and re-layouts, on_device(): zonal_parts = zonal_parts.astype(jnp.bfloat16).reshape(1, 2 * M, columns)  24.6 us
    unnamed x13, local copies, waits for them, and re-layouts  24.6 us
  transfers between devices with their start and end apart: 2, of which 2 were waited for; matrix products, arithmetic and copies ran while one was open for 0% of the time, Pallas kernels for 0%

commit v1 on v0

--- a/solution.py
+++ b/solution.py
@@ -57,7 +57,12 @@
         "mrfn,msan->smrfa", weighted, legendre_view, preferred_element_type=jnp.float32
     )
     synthesis = synthesis.astype(jnp.bfloat16).reshape(sources, 2 * own_waves, columns)
-    returned = lax.all_to_all(synthesis, "space", split_axis=0, concat_axis=1, tiled=True)
+    returned = jnp.concatenate(
+        lax.all_to_all(
+            jnp.stack(jnp.split(synthesis, lax.axis_size("space"), axis=0)), "space", 0, 0
+        ),
+        axis=1,
+    )
     spread = lax.dot_general(
         returned.reshape(2 * M, columns),
         fourier,

time: 607 us -> 636 us (1.048)
  local copies, waits for them, and re-layouts: 163 us -> 190 us
    another operation x0 -> x18, local copies, waits for them, and re-layouts: none -> 36.3 us  [the longest x17 29.8 us: on_device(): jnp.stack(jnp.split(synthesis, lax.axis_size('space'), axis=0))]
    reshape x2 -> x0, local copies, waits for them, and re-layouts: 29.1 us -> none  [the longest x1 22.6 us: on_device(): synthesis.astype(jnp.bfloat16).reshape(sources, 2 * own_waves, columns)]
    split x0 -> x17, local copies, waits for them, and re-layouts: none -> 26.3 us  [on_device(): jnp.split(synthesis, lax.axis_size('space'), axis=0)]
    convert_element_type x1 -> x0, local copies, waits for them, and re-layouts: 15.9 us -> none  [on_device(): synthesis.astype(jnp.bfloat16).reshape(sources, 2 * own_waves, columns)]
    unnamed x13 -> x54, local copies, waits for them, and re-layouts: 24.6 us -> 35.5 us
where the time goes in v1:
time: 636 us; the launch traced here: 625 us
  local copies, waits for them, and re-layouts  190 us (30%)
  waiting for transfers between devices  163 us (26%)
  blocking collectives  112 us (18%)
  matrix products  91.3 us (14%)
  other arithmetic  45.6 us (7%)
  between operations  14.6 us (2%)
  starting transfers between devices  7.61 us (1%)
    all_to_all x1, blocking collectives, on_device(): lax.all_to_all(jnp.stack(jnp.split(synthesis, lax.axis_size('space'), axi...  112 us
    psum x1, waiting for transfers between devices, on_device(): lax.psum(partial_value.astype(jnp.bfloat16), 'mem').astype(jnp.float32)  86.7 us
    all_to_all x1, waiting for transfers between devices, on_device(): lax.all_to_all(zonal_parts, 'space', split_axis=1, concat_axis=0, tiled=T...  76.7 us
    unnamed x54, local copies, waits for them, and re-layouts  35.5 us
    dot_general x1, matrix products, on_device(): lifted = jnp.einsum('jl,kjac->klac', modes, spread, precision=highest)  31 us
    another operation x17, local copies, waits for them, and re-layouts, on_device(): jnp.stack(jnp.split(synthesis, lax.axis_size('space'), axis=0))  29.8 us
    unnamed x1, other arithmetic  27.4 us
    all_to_all x1, local copies, waits for them, and re-layouts, on_device(): lax.all_to_all(zonal_parts, 'space', split_axis=1, concat_axis=0, tiled=T...  27.3 us
  transfers between devices with their start and end apart: 2, of which 2 were waited for; matrix products, arithmetic and copies ran while one was open for 0% of the time, Pallas kernels for 0%

profile of v1, /device:TPU:0, one launch (start us, length us, event | category | flops | bytes accessed | tf_op | source)
XLA Modules:
  0.0 625.1 jit_solution(16767676550870740987)
XLA Ops:
  6.5 12.9 %sine_negate_fusion = (f32[1536,512,1]{1,0,2:T(8,128)S(1)}, f32[1536,512,1]{1,0,2:T(8,128)S(1)}) fusion(), kind=kLoop, calls=%fused_computation.23 | loop fusion | flops 7864320 | bytes 6291456 | tf_op jit(solution)/shard_map/neg | solution.py:19
  22.0 7.4 %copy.57 = bf16[1536,512,2]{0,2,1:T(2,128)(2,1)S(1)} copy(bf16[1536,512,2]{1,0,2:T(8,128)(2,1)} %fusion.7) | data formatting | bytes 6291456 | tf_op jit(solution)/shard_map/convert_element_type | solution.py:20
  32.1 3.7 copy.58
  35.9 23.7 %convert_bitcast_fusion.1 = bf16[4,16,32,1536]{3,1,2,0:T(8,128)(2,1)S(1)} fusion(f32[32,32,1536]{2,0,1:T(8,128)S(1)} %copy.58, bf16[4,32,32,1536]{3,2,1,0:T(8,128)(2,1)} %param.6, f32[16,32]{1,0:T(8,128)S(1)} %copy-done), kind=kOutput, calls=%fused_computation.13 | convolution fusion | flops 1223688192 | bytes 25167872 | tf_op jit(solution)/shard_map/jl,klac->kjac/dot_general | solution.py:32
  59.5 3.5 copy.59
  63.1 6.9 %convert_bitcast_fusion.2 = bf16[1,1024,2048]{2,1,0:T(8,128)(2,1)S(1)} fusion(bf16[1536,1024]{0,1:T(8,128)(2,1)S(1)} %copy-done.1, bf16[2048,1536]{1,0:T(8,128)(2,1)S(1)} %bitcast.90), kind=kOutput, calls=%fused_computation.19 | convolution fusion | flops 6444548096 | bytes 13631488 | tf_op jit(solution)/shard_map/dot_general | solution.py:35
  70.0 24.7 %copy.112 = bf16[1,1024,2048]{2,0,1:T(2,128)(2,1)} copy(bf16[1,1024,2048]{2,1,0:T(8,128)(2,1)S(1)} %convert_bitcast_fusion.2) | data formatting | bytes 8388608 | tf_op jit(solution)/shard_map/reshape | solution.py:41
  95.2 27.4 %reduce.2 = bf16[1024,2048]{1,0:T(8,128)(2,1)} reduce(bf16[1024,1,2048]{2,1,0:T(2,128)(2,1)} %bitcast.86, bf16[]{:T(256)} %broadcast.88), dimensions={1}, to_apply=%bitcast.84.reduce_sub_computation | reduce | bytes 8388610
  122.6 11.4 %reshape.138 = bf16[16,2,65536]{2,1,0:T(2,128)(2,1)} reshape(bf16[1024,2048]{1,0:T(8,128)(2,1)} %reduce.2) | data formatting | bytes 8388608
  133.9 7.6 %all-to-all-start = ((bf16[16,2,65536]{2,1,0:T(2,128)(2,1)}), bf16[16,2,65536]{2,1,0:T(2,128)(2,1)}, u32[]{:S(2)}, u32[]{:S(2)}) async-start(bf16[16,2,65536]{2,1,0:T(2,128)(2,1)} %reshape.138), calls=%async_computation | async-start | bytes 8388608 | tf_op jit(solution)/shard_map/all_to_all | solution.py:49
  142.3 76.7 %all-to-all-done = bf16[16,2,65536]{2,1,0:T(2,128)(2,1)} async-done(((bf16[16,2,65536]{2,1,0:T(2,128)(2,1)}), bf16[16,2,65536]{2,1,0:T(2,128)(2,1)}, u32[]{:S(2)}, u32[]{:S(2)}) %all-to-all-start) | async-done | bytes 4194336 | tf_op jit(solution)/shard_map/all_to_all | solution.py:49
  219.0 12.7 %reshape.139 = bf16[1024,1,2048]{2,1,0:T(2,128)(2,1)} reshape(bf16[16,2,65536]{2,1,0:T(2,128)(2,1)} %all-to-all-done) | data formatting | bytes 8388608
  231.8 27.3 %bitcast_reduce_fusion = bf16[1024,2048]{1,0:T(8,128)(2,1)} fusion(bf16[1024,1,2048]{2,1,0:T(2,128)(2,1)} %reshape.139), kind=kLoop, calls=%fused_computation.53 | loop fusion | bytes 8388608 | tf_op jit(solution)/shard_map/all_to_all | solution.py:49
  259.1 19.5 %reshape.129 = bf16[16,32,2,64,32]{4,3,2,1,0:T(8,128)(2,1)} reshape(bf16[1024,2048]{1,0:T(8,128)(2,1)} %bitcast_reduce_fusion) | data formatting | bytes 8388608 | tf_op jit(solution)/shard_map/reshape | solution.py:50
  278.5 10.1 %fusion.2 = f32[32,2,64,256,1]{3,2,0,1,4:T(8,128)S(1)} fusion(bf16[16,32,2,64,32]{4,3,2,1,0:T(8,128)(2,1)} %reshape.129, bf16[32,16,32,256,1]{3,2,1,0,4:T(8,128)(2,1)} %bitcast.88), kind=kOutput, calls=%fused_computation.4 | convolution fusion | flops 1073741824 | bytes 16777216 | tf_op jit(solution)/shard_map/smrfa,msan->mrfn/dot_general | solution.py:52
  288.6 10.1 %convert_bitcast_fusion = bf16[16,32,2,64,32]{3,4,0,2,1:T(8,128)(2,1)} fusion(bf16[32,16,32,256,1]{3,2,1,4,0:T(8,128)(2,1)} %bitcast.89, f32[32,2,64,256,1]{3,2,0,1,4:T(8,128)S(1)} %fusion.2, f32[32,256]{1,0:T(8,128)S(1)} %fusion.21), kind=kOutput, calls=%fused_computation.9 | convolution fusion | flops 1077936128 | bytes 16809984 | tf_op jit(solution)/shard_map/mrfn,msan->smrfa/dot_general | solution.py:56
  298.7 6.3 %fusion.24 = (bf16[1,32,2,64,32]{3,4,0,2,1:T(8,128)(2,1)S(1)}, bf16[1,32,2,64,32]{3,4,0,2,1:T(8,128)(2,1)S(1)}, bf16[1,32,2,64,32]{3,4,0,2,1:T(8,128)(2,1)S(1)},...) fusion(bf16[16,32,2,64,32]{3,4,0,2,1:T(8,128)(2,1)} %convert_bi, ...), kind=kLoop, calls=%fused_computation.52 | loop fusion | bytes 8388608 | tf_op jit(solution)/shard_map/split | solution.py:62
  365.9 112.3 %all_to_all.14 = bf16[16,1,64,2048]{3,2,1,0:T(8,128)(2,1)} all-to-all(bf16[16,1,64,2048]{3,2,1,0:T(8,128)(2,1)} %constant_dynamic-update-slice_fusion), channel_id=1, replica_groups=mesh['space'=16,'mem'=2] {'space'}, dimensions={0} | all-to-all | bytes 8388608 | tf_op jit(solution)/shard_map/all_to_all | solution.py:61
  478.1 6.6 %copy.79 = bf16[1024,2048]{0,1:T(8,128)(2,1)} copy(bf16[1024,2048]{1,0:T(8,128)(2,1)} %bitcast.87) | data formatting | bytes 8388608 | tf_op jit(solution)/shard_map/reshape;reshape | solution.py:67
  484.7 9.5 %fusion.9 = f32[4,16,32,1536]{3,1,2,0:T(8,128)S(1)} fusion(bf16[4,16,32,1024]{3,2,1,0:T(8,128)(2,1)} %bitcast.91, bf16[1536,1024]{0,1:T(8,128)(2,1)S(1)} %copy-done.2), kind=kOutput, calls=%fused_computation.17 | convolution fusion | flops 6442450944 | bytes 19922944 | tf_op jit(solution)/shard_map/dot_general | solution.py:66
  494.2 31.0 %fusion.1 = bf16[32,32,1536]{2,0,1:T(8,128)(2,1)} fusion(f32[4,16,32,1536]{3,1,2,0:T(8,128)S(1)} %fusion.9, bf16[4,32,32,1536]{3,2,1,0:T(8,128)(2,1)} %param.6, f32[16,32]{1,0:T(8,128)S(1)} %copy-done), kind=kOutput, calls=%fused_computation.3 | convolution fusion | flops 1225261056 | bytes 28313600 | tf_op jit(solution)/shard_map/jl,kjac->klac/dot_general | solution.py:73
  525.3 86.7 %all-reduce.2.cloned.1.call-done = bf16[32,32,1536]{2,0,1:T(8,128)(2,1)} async-done(((bf16[32,32,1536]{2,0,1:T(8,128)(2,1)}), bf16[32,32,1536]{2,0,1:T(8,128)(2,1)}) %all-reduce.2.cloned.1.call-update) | async-done | bytes 3145744 | tf_op jit(solution)/shard_map/psum | solution.py:75
  612.0 2.7 multiply_convert_fusion
  614.6 3.4 copy.82
  (91 shorter events, 66.5 us)
Async XLA Ops:
  6.5 29.3 %copy-start = (f32[16,32]{1,0:T(8,128)S(1)}, f32[16,32]{1,0:T(8,128)}, u32[]{:S(2)}) copy-start(f32[16,32]{1,0:T(8,128)} %param.8) | copy-start | bytes 6148
  59.5 3.5 copy-start.1
  133.9 8.3 %copy-start.17 = (f32[32,256]{1,0:T(8,128)S(1)}, f32[32,256]{1,0:T(8,128)}, u32[]{:S(2)}) copy-start(f32[32,256]{1,0:T(8,128)} %param.10) | copy-start | bytes 98308
  133.9 85.1 %all-to-all-start = ((bf16[16,2,65536]{2,1,0:T(2,128)(2,1)}), bf16[16,2,65536]{2,1,0:T(2,128)(2,1)}, u32[]{:S(2)}, u32[]{:S(2)}) async-start(bf16[16,2,65536]{2,1,0:T(2,128)(2,1)} %reshape.138), calls=%async_computation | async-start | bytes 8388608 | tf_op jit(solution)/shard_map/all_to_all | solution.py:49
  141.5 470.5 %all-reduce.2.cloned.1.call-start = ((), (), s32[]{:S(2)}) async-start(), calls=%async_computation.2 | async-start | bytes 6291456 | tf_op jit(solution)/shard_map/psum | solution.py:75
  348.2 7.5 %copy-start.3 = (bf16[1,1,64,2048]{3,2,1,0:T(8,128)(2,1)S(1)}, bf16[1,1,64,2048]{3,2,1,0:T(8,128)(2,1)}, u32[]{:S(2)}) copy-start(bf16[1,1,64,2048]{3,2,1,0:T(8,128)(2,1)} %stack.59) | copy-start | bytes 786436
  348.2 8.2 %copy-start.4 = (bf16[1,1,64,2048]{3,2,1,0:T(8,128)(2,1)S(1)}, bf16[1,1,64,2048]{3,2,1,0:T(8,128)(2,1)}, u32[]{:S(2)}) copy-start(bf16[1,1,64,2048]{3,2,1,0:T(8,128)(2,1)} %stack.60) | copy-start | bytes 786436
  348.2 8.9 %copy-start.5 = (bf16[1,1,64,2048]{3,2,1,0:T(8,128)(2,1)S(1)}, bf16[1,1,64,2048]{3,2,1,0:T(8,128)(2,1)}, u32[]{:S(2)}) copy-start(bf16[1,1,64,2048]{3,2,1,0:T(8,128)(2,1)} %stack.61) | copy-start | bytes 786436
  350.2 7.7 %copy-start.6 = (bf16[1,1,64,2048]{3,2,1,0:T(8,128)(2,1)S(1)}, bf16[1,1,64,2048]{3,2,1,0:T(8,128)(2,1)}, u32[]{:S(2)}) copy-start(bf16[1,1,64,2048]{3,2,1,0:T(8,128)(2,1)} %stack.62) | copy-start | bytes 786436
  350.6 8.0 %copy-start.7 = (bf16[1,1,64,2048]{3,2,1,0:T(8,128)(2,1)S(1)}, bf16[1,1,64,2048]{3,2,1,0:T(8,128)(2,1)}, u32[]{:S(2)}) copy-start(bf16[1,1,64,2048]{3,2,1,0:T(8,128)(2,1)} %stack.63) | copy-start | bytes 786436
  350.6 8.7 %copy-start.8 = (bf16[1,1,64,2048]{3,2,1,0:T(8,128)(2,1)S(1)}, bf16[1,1,64,2048]{3,2,1,0:T(8,128)(2,1)}, u32[]{:S(2)}) copy-start(bf16[1,1,64,2048]{3,2,1,0:T(8,128)(2,1)} %stack.64) | copy-start | bytes 786436
  353.0 7.0 %copy-start.9 = (bf16[1,1,64,2048]{3,2,1,0:T(8,128)(2,1)S(1)}, bf16[1,1,64,2048]{3,2,1,0:T(8,128)(2,1)}, u32[]{:S(2)}) copy-start(bf16[1,1,64,2048]{3,2,1,0:T(8,128)(2,1)} %stack.65) | copy-start | bytes 786436
  353.0 7.8 %copy-start.10 = (bf16[1,1,64,2048]{3,2,1,0:T(8,128)(2,1)S(1)}, bf16[1,1,64,2048]{3,2,1,0:T(8,128)(2,1)}, u32[]{:S(2)}) copy-start(bf16[1,1,64,2048]{3,2,1,0:T(8,128)(2,1)} %stack.66) | copy-start | bytes 786436
  354.9 6.6 %copy-start.11 = (bf16[1,1,64,2048]{3,2,1,0:T(8,128)(2,1)S(1)}, bf16[1,1,64,2048]{3,2,1,0:T(8,128)(2,1)}, u32[]{:S(2)}) copy-start(bf16[1,1,64,2048]{3,2,1,0:T(8,128)(2,1)} %stack.67) | copy-start | bytes 786436
  354.9 7.3 %copy-start.12 = (bf16[1,1,64,2048]{3,2,1,0:T(8,128)(2,1)S(1)}, bf16[1,1,64,2048]{3,2,1,0:T(8,128)(2,1)}, u32[]{:S(2)}) copy-start(bf16[1,1,64,2048]{3,2,1,0:T(8,128)(2,1)} %stack.68) | copy-start | bytes 786436
  354.9 8.0 %copy-start.13 = (bf16[1,1,64,2048]{3,2,1,0:T(8,128)(2,1)S(1)}, bf16[1,1,64,2048]{3,2,1,0:T(8,128)(2,1)}, u32[]{:S(2)}) copy-start(bf16[1,1,64,2048]{3,2,1,0:T(8,128)(2,1)} %stack.69) | copy-start | bytes 786436
  354.9 8.8 %copy-start.14 = (bf16[1,1,64,2048]{3,2,1,0:T(8,128)(2,1)S(1)}, bf16[1,1,64,2048]{3,2,1,0:T(8,128)(2,1)}, u32[]{:S(2)}) copy-start(bf16[1,1,64,2048]{3,2,1,0:T(8,128)(2,1)} %stack.70) | copy-start | bytes 786436
  355.0 9.5 %copy-start.15 = (bf16[1,1,64,2048]{3,2,1,0:T(8,128)(2,1)S(1)}, bf16[1,1,64,2048]{3,2,1,0:T(8,128)(2,1)}, u32[]{:S(2)}) copy-start(bf16[1,1,64,2048]{3,2,1,0:T(8,128)(2,1)} %stack.71) | copy-start | bytes 786436
  355.0 10.2 %copy-start.16 = (bf16[1,1,64,2048]{3,2,1,0:T(8,128)(2,1)S(1)}, bf16[1,1,64,2048]{3,2,1,0:T(8,128)(2,1)}, u32[]{:S(2)}) copy-start(bf16[1,1,64,2048]{3,2,1,0:T(8,128)(2,1)} %stack.72) | copy-start | bytes 786436
  478.1 6.6 %copy-start.2 = (bf16[1536,1024]{0,1:T(8,128)(2,1)S(1)}, bf16[1536,1024]{0,1:T(8,128)(2,1)}, u32[]{:S(2)}) copy-start(bf16[1536,1024]{0,1:T(8,128)(2,1)} %convert_element_type.69) | copy-start | bytes 9437188
Sparse Core Ops, SparseCore 0:
  525.4 86.5 all-reduce.1
